TPU v7x, 32 devices: a whole 2x2x4 slice. The times are simulated.
32 devices in a mesh: shard: 4 (over z), tensor: 4 (over x, core), section: 2 (over y).
Axes of the slice: x: 2, y: 2, z: 4, core: 2. Of those that a mesh axis runs over, the one named last changes fastest.
Arguments:
- hidden_acts: bfloat16 [2, 10240, 4096], P('section', 'shard', 'tensor'), may hold values from -8 to 8
- out_grads: bfloat16 [2, 10240, 1024], P('section', 'shard'), may hold values from -8 to 8
- errors: float32 [2, 4, 1024, 4096], P('section', 'shard', None, 'tensor'), may hold values from -3 to 3
- factors: float32 [2, 32, 4096], P('section', None, 'tensor'), may hold values from -6 to 6
- whiten: float32 [2, 2, 32, 32], P('section'), may hold values from -1.5 to 3
- momentum: float32 [2, 1024, 4096], P('section', 'shard', 'tensor'), may hold values from -3 to 3
- master: float32 [2, 1024, 4096], P('section', 'shard', 'tensor'), may hold values from -3 to 3
- table: bfloat16 [32768, 1024], P(('shard', 'section'), 'tensor'), may hold values from -5 to 5
- touched_ids: int32 [1024], P(('shard', 'section')), may hold values from 0 to 32767, as said below
- touched_grads: bfloat16 [1024, 1024], P(('shard', 'section'), 'tensor'), may hold values from -5 to 5
Outputs:
- new_errors: float32 [2, 4, 1024, 4096], P('section', 'shard', None, 'tensor')
- new_factors: float32 [2, 32, 4096], P('section', None, 'tensor')
- new_momentum: float32 [2, 1024, 4096], P('section', 'shard', 'tensor')
- new_master: float32 [2, 1024, 4096], P('section', 'shard', 'tensor')
- new_weights: bfloat16 [2, 1024, 4096], P('section', None, 'tensor')
- new_table: bfloat16 [32768, 1024], P(('shard', 'section'), 'tensor')
Inputs may be any that keep to these rules, and one draw needn't show every extreme that they name: `touched_ids`: the 128 ids of one device of shard and section name at most 32 rows in each block of 4096 vocabulary rows; in every draw one block receives exactly 32 rows from every device.
All inputs are finite; a program needn't handle non-finite values.
Results may differ from a plain program's by a relative error of at most 0.0036.
Values may be sent and summed in bfloat16 or wider, within the bound.
A program may use at most 128 MiB of HBM per device.

v0:
```python
import jax
import jax.numpy as jnp
from jax import lax
from jax.sharding import PartitionSpec as P

D = 1024
FF = 4096
ROUNDS = 2
epsilon = 1e-06
momentum_decay = 0.9
learn_rate = 0.1
embed_rate = 0.25
clip_level = 0.03
highest = lax.Precision.HIGHEST


def on_device(
    hidden_acts,
    out_grads,
    errors,
    factors,
    whiten,
    momentum,
    master,
    table,
    touched_ids,
    touched_grads,
):
    shards = lax.axis_size("shard")
    grad_block = lax.dot_general(
        out_grads[0], hidden_acts[0], (((0,), (0,)), ((), ())), preferred_element_type=jnp.float32
    )
    rounded = lax.optimization_barrier(grad_block.astype(jnp.bfloat16))
    corrected = rounded.astype(jnp.float32) + errors[0, 0]
    right_part = factors[0]
    rank_count = right_part.shape[0]
    left_unit = None
    for power_round in range(ROUNDS):
        left_part = lax.dot_general(
            right_part,
            corrected,
            (((1,), (1,)), ((), ())),
            precision=highest,
            preferred_element_type=jnp.float32,
        )
        left_sum = lax.psum(left_part, ("shard", "tensor"))
        whitened = jnp.dot(whiten[0, power_round].T, left_sum, precision=highest)
        scaling = lax.rsqrt(jnp.sum(whitened * whitened) / rank_count + epsilon)
        left_unit = whitened * scaling
        right_local = jnp.dot(left_unit, corrected, precision=highest)
        right_part = lax.psum(right_local, "shard") / shards
    gram_left = jnp.dot(left_unit, left_unit.T, precision=highest)
    gram_right = jnp.dot(right_part, right_part.T, precision=highest)
    total_squares = lax.psum(jnp.sum(gram_left * gram_right), ("tensor", "section"))
    approx = lax.dot_general(
        left_unit,
        right_part,
        (((0,), (0,)), ((), ())),
        precision=highest,
        preferred_element_type=jnp.float32,
    )
    new_errors = (corrected - approx)[None, None]
    entries = lax.axis_size("section") * D * FF
    spread = jnp.sqrt(total_squares / entries + epsilon)
    clip_factor = jnp.minimum(1.0, clip_level / spread)
    rows_own = momentum.shape[1]
    row_start = lax.axis_index("shard") * rows_own
    approx_rows = lax.dynamic_slice_in_dim(approx, row_start, rows_own, 0)
    new_momentum = momentum_decay * momentum + clip_factor * approx_rows[None]
    new_master = master - learn_rate * new_momentum
    new_weights = lax.all_gather(new_master.astype(jnp.bfloat16), "shard", axis=1, tiled=True)
    new_factors = right_part[None]
    vocab_rows = table.shape[0]
    table_width = table.shape[1]
    first_row = lax.axis_index(("shard", "section")) * vocab_rows
    recv_rows, recv_ids = (
        lax.all_gather(touched_grads, ("shard", "section"), axis=0, tiled=True),
        lax.all_gather(touched_ids, ("shard", "section"), axis=0, tiled=True),
    )
    local_index = recv_ids - first_row
    inside = (local_index >= 0) & (local_index < vocab_rows)
    target = jnp.where(inside, local_index, vocab_rows)
    table_grad = (
        jnp.zeros((vocab_rows, table_width), jnp.float32)
        .at[target]
        .add(recv_rows.astype(jnp.float32), mode="drop")
    )
    new_table = (table.astype(jnp.float32) - embed_rate * table_grad).astype(jnp.bfloat16)
    return (new_errors, new_factors, new_momentum, new_master, new_weights, new_table)


def solution(mesh):
    in_specs = (
        P("section", "shard", "tensor"),
        P("section", "shard", None),
        P("section", "shard", None, "tensor"),
        P("section", None, "tensor"),
        P("section", None, None, None),
        P("section", "shard", "tensor"),
        P("section", "shard", "tensor"),
        P(("shard", "section"), "tensor"),
        P(("shard", "section")),
        P(("shard", "section"), "tensor"),
    )
    out_specs = (
        P("section", "shard", None, "tensor"),
        P("section", None, "tensor"),
        P("section", "shard", "tensor"),
        P("section", "shard", "tensor"),
        P("section", None, "tensor"),
        P(("shard", "section"), "tensor"),
    )
    return jax.shard_map(
        on_device, mesh=mesh, in_specs=in_specs, out_specs=out_specs, check_vma=False
    )
```

profile of v0, /device:TPU:0, one launch (start us, length us, event | category | flops | bytes accessed | tf_op | source)
XLA Modules:
  0.0 398.0 jit_solution(17824651592674097183)
XLA Ops:
  7.2 0.0 copy-start
  7.2 0.0 all-reduce.5.cloned.1.call-start
  7.2 0.0 copy-start.1
  7.2 9.3 %fusion.5 = bf16[1024,1024]{1,0:T(8,128)(2,1)S(1)} fusion(bf16[1,2560,1024]{2,1,0:T(8,128)(2,1)} %param.10, bf16[1,2560,1024]{2,1,0:T(8,128)(2,1)} %param.11), kind=kOutput, calls=%fused_computation.9 | convolution fusion | flops 5369757696 | bytes 12582912 | tf_op jit(solution)/shard_map/dot_general | solution.py:30
  16.5 0.0 copy-done
  16.5 0.0 copy-done.1
  16.5 0.0 copy-start.9
  16.6 4.7 %convolution_bitcast_fusion = f32[32,1024]{1,0:T(8,128)} fusion(f32[1,32,1024]{2,1,0:T(8,128)S(1)} %copy-done, f32[1,1,1024,1024]{3,2,1,0:T(8,128)S(1)} %copy-done.1, bf16[1024,1024]{1,0:T(8,128)(2,1)S(1)} %fusion.5), kind=kOutput, calls=%fused_computation.10 | convolution fusion | flops 404750336 | bytes 6553600 | tf_op jit(solution)/shard_map/dot_general | solution.py:39
  21.2 0.0 all-reduce.5.cloned.1.call-update
  21.3 0.0 all-reduce.7.cloned.1.call-start
  21.3 89.8 %all-reduce.5.cloned.1.call-done = f32[32,1024]{1,0:T(8,128)} async-done(((f32[32,1024]{1,0:T(8,128)}), f32[32,1024]{1,0:T(8,128)}) %all-reduce.5.cloned.1.call-update) | async-done | bytes 131088 | tf_op jit(solution)/shard_map/psum | solution.py:46
  111.1 0.0 copy-done.9
  111.1 1.8 multiply_reduce_fusion.1
  113.7 5.6 %fusion.15 = f32[32,1024]{1,0:T(8,128)} fusion(f32[1024,32]{0,1:T(8,128)S(1)} %get-tuple-element.10, f32[]{:T(128)S(6)} %rsqrt.7, f32[1,1,1024,1024]{3,2,1,0:T(8,128)} %param.12, bf16[1024,1024]{1,0:T(8,128)(2,1)S(1)} %fusion.5), kind=kOutput, calls=%fused_computation.20 | convolution fusion | flops 404783104 | bytes 6553604 | tf_op jit(solution)/shard_map/dot_general | solution.py:50
  119.2 0.0 all-reduce.7.cloned.1.call-update
  119.2 0.0 all-reduce.9.cloned.1.call-start
  119.3 36.2 %all-reduce.7.cloned.1.call-done = f32[32,1024]{1,0:T(8,128)} async-done(((f32[32,1024]{1,0:T(8,128)}), f32[32,1024]{1,0:T(8,128)}) %all-reduce.7.cloned.1.call-update) | async-done | bytes 131088 | tf_op jit(solution)/shard_map/psum | solution.py:51
  155.5 6.8 %fusion.13 = f32[32,1024]{1,0:T(8,128)} fusion(f32[32,1024]{1,0:T(8,128)} %all-reduce.7.cloned.1.call-done, f32[1,1,1024,1024]{3,2,1,0:T(8,128)} %param.12, bf16[1024,1024]{1,0:T(8,128)(2,1)S(1)} %fusion.5), kind=kOutput, calls=%fused_computation.18 | convolution fusion | flops 404783104 | bytes 6553600 | tf_op jit(solution)/shard_map/dot_general | solution.py:39
  162.2 0.0 all-reduce.9.cloned.1.call-update
  162.3 0.2 all-reduce.11.cloned.1.call-start
  162.5 86.6 %all-reduce.9.cloned.1.call-done = f32[32,1024]{1,0:T(8,128)} async-done(((f32[32,1024]{1,0:T(8,128)}), f32[32,1024]{1,0:T(8,128)}) %all-reduce.9.cloned.1.call-update) | async-done | bytes 131088 | tf_op jit(solution)/shard_map/psum | solution.py:46
  249.1 1.8 multiply_reduce_fusion
  251.6 0.0 copy-start.6
  251.6 5.6 %fusion.23 = f32[32,1024]{1,0:T(8,128)} fusion(f32[1024,32]{0,1:T(8,128)S(1)} %get-tuple-element.12, f32[]{:T(128)S(6)} %rsqrt.8, f32[1,1,1024,1024]{3,2,1,0:T(8,128)} %param.12, bf16[1024,1024]{1,0:T(8,128)(2,1)S(1)} %fusion.5), kind=kOutput, calls=%fused_computation.30 | convolution fusion | flops 404783104 | bytes 6553604 | tf_op jit(solution)/shard_map/dot_general | solution.py:50
  257.2 0.0 all-reduce.11.cloned.1.call-update
  257.3 0.0 all-gather.3.cloned.1.call-start
  257.3 0.2 fusion.20
  257.6 36.0 %all-reduce.11.cloned.1.call-done = f32[32,1024]{1,0:T(8,128)} async-done(((f32[32,1024]{1,0:T(8,128)}), f32[32,1024]{1,0:T(8,128)}) %all-reduce.11.cloned.1.call-update) | async-done | bytes 131088 | tf_op jit(solution)/shard_map/psum | solution.py:51
  293.6 1.8 fusion.11
  295.4 14.0 %psum.39 = f32[]{:T(128)} all-reduce(f32[]{:T(128)} %fusion.11), channel_id=1, replica_groups=mesh['shard'=4,'tensor'=4,'section'=2] {'tensor','section'}, use_global_device_ids=true, to_apply=%region_7.0 | all-reduce | flops 1 | bytes 8 | tf_op jit(solution)/shard_map/psum | solution.py:54
  310.1 0.0 copy-start.7
  310.1 4.5 %fusion.18 = f32[1024,1024]{1,0:T(8,128)S(1)} fusion(f32[32,1024]{1,0:T(8,128)} %all-reduce.11.cloned.1.call-done, f32[1024,32]{0,1:T(8,128)S(1)} %get-tuple-element.12, f32[]{:T(128)S(6)} %rsqrt.8), kind=kOutput, calls=%fused_computation.25 | convolution fusion | flops 402718720 | bytes 4456452 | tf_op jit(solution)/shard_map/dot_general | solution.py:55
  314.6 0.0 copy-start.3
  314.6 2.0 copy-done.3
  316.6 0.0 copy-done.6
  316.6 0.0 copy-done.7
  316.6 1.9 fusion.41
  318.5 0.0 all-gather.3.cloned.1.call-update
  318.6 0.0 copy-done.10
  318.6 18.6 %all-gather = s32[8,1,128]{2,1,0:T(1,128)S(1)} all-gather(s32[1,1,128]{2,1,0:T(1,128)S(1)} %bitcast.48), channel_id=1, replica_groups=mesh['shard'=4,'tensor'=4,'section'=2] {'shard','section'}, dimensions={0}, use_global_device_ids=true | all-gather | bytes 4608 | tf_op jit(solution)/shard_map/all_gather | solution.py:78
  337.2 0.0 copy-done.8
  337.2 33.2 %all_gather.11 = bf16[1024,256]{1,0:T(8,128)(2,1)S(1)} all-gather(bf16[128,256]{1,0:T(8,128)(2,1)S(1)} %copy-done.8), channel_id=1, replica_groups=mesh['shard'=4,'tensor'=4,'section'=2] {'shard','section'}, dimensions={0}, use_global_device_ids=true | all-gather | bytes 589824 | tf_op jit(solution)/shard_map/all_gather | solution.py:77
  370.3 8.3 %scatter_custom_fusion = f32[4096,256]{1,0:T(8,128)} fusion(s32[1024]{0:T(1024)S(1)} %compare_select_fusion, f32[]{:T(128)} %constant.16.clone.1, bf16[1024,256]{1,0:T(8,128)(2,1)S(1)} %all_gather.11), kind=kCustom, calls=%fused_computation.7 | custom fusion | flops 524288 | bytes 4718596 | tf_op jit(solution)/shard_map/scatter-add | solution.py:86
  378.6 4.8 %subtract_convert_fusion = bf16[4096,256]{1,0:T(8,128)(2,1)} fusion(f32[4096,256]{1,0:T(8,128)} %scatter_custom_fusion, bf16[4096,256]{1,0:T(8,128)(2,1)} %param.17), kind=kLoop, calls=%fused_computation.5 | loop fusion | flops 4194304 | bytes 8388608 | tf_op jit(solution)/shard_map/convert_element_type | solution.py:88
  383.4 0.7 multiply_bitcast_fusion
  384.1 0.6 copy-done.4
  384.7 3.6 subtract_bitcast_fusion
  388.3 3.1 copy.21
  (10 shorter events, 0.0 us)
Async XLA Ops:
  7.2 9.4 %copy-start = (f32[1,32,1024]{2,1,0:T(8,128)S(1)}, f32[1,32,1024]{2,1,0:T(8,128)}, u32[]{:S(2)}) copy-start(f32[1,32,1024]{2,1,0:T(8,128)} %param.13) | copy-start | bytes 393220
  7.2 103.9 %all-reduce.5.cloned.1.call-start = ((), (), s32[]{:S(2)}) async-start(), calls=%async_computation | async-start | bytes 262144 | tf_op jit(solution)/shard_map/psum | solution.py:46
  7.2 9.3 %copy-start.1 = (f32[1,1,1024,1024]{3,2,1,0:T(8,128)S(1)}, f32[1,1,1024,1024]{3,2,1,0:T(8,128)}, u32[]{:S(2)}) copy-start(f32[1,1,1024,1024]{3,2,1,0:T(8,128)} %param.12) | copy-start | bytes 12582916
  16.5 94.6 %copy-start.9 = (f32[1,2,32,32]{3,2,1,0:T(8,128)S(1)}, f32[1,2,32,32]{3,2,1,0:T(8,128)}, u32[]{:S(2)}) copy-start(f32[1,2,32,32]{3,2,1,0:T(8,128)} %param.14) | copy-start | bytes 24580
  21.3 134.2 %all-reduce.7.cloned.1.call-start = ((), (), s32[]{:S(2)}) async-start(), calls=%async_computation.1 | async-start | bytes 262144 | tf_op jit(solution)/shard_map/psum | solution.py:51
  119.2 129.8 %all-reduce.9.cloned.1.call-start = ((), (), s32[]{:S(2)}) async-start(), calls=%async_computation.2 | async-start | bytes 262144 | tf_op jit(solution)/shard_map/psum | solution.py:46
  162.3 131.3 %all-reduce.11.cloned.1.call-start = ((), (), s32[]{:S(2)}) async-start(), calls=%async_computation.3 | async-start | bytes 262144 | tf_op jit(solution)/shard_map/psum | solution.py:51
  251.6 65.0 %copy-start.6 = (f32[1,256,1024]{2,1,0:T(8,128)S(1)}, f32[1,256,1024]{2,1,0:T(8,128)}, u32[]{:S(2)}) copy-start(f32[1,256,1024]{2,1,0:T(8,128)} %param.16) | copy-start | bytes 3145732
  257.3 131.1 %all-gather.3.cloned.1.call-start = ((), (), s32[]{:S(2)}) async-start(), calls=%async_computation.4 | async-start | bytes 2621440 | tf_op jit(solution)/shard_map/all_gather | solution.py:71
  310.1 6.5 %copy-start.7 = (f32[1,256,1024]{2,1,0:T(8,128)S(1)}, f32[1,256,1024]{2,1,0:T(8,128)}, u32[]{:S(2)}) copy-start(f32[1,256,1024]{2,1,0:T(8,128)} %param.15) | copy-start | bytes 3145732
  314.6 2.0 copy-start.3
  316.6 2.0 copy-start.10
  316.6 20.6 %copy-start.8 = (bf16[128,256]{1,0:T(8,128)(2,1)S(1)}, bf16[128,256]{1,0:T(8,128)(2,1)}, u32[]{:S(2)}) copy-start(bf16[128,256]{1,0:T(8,128)(2,1)} %param.19) | copy-start | bytes 196612
  370.3 13.1 %copy-start.5 = (f32[32,1024]{1,0:T(8,128)S(1)}, f32[32,1024]{1,0:T(8,128)}, u32[]{:S(2)}) copy-start(f32[32,1024]{1,0:T(8,128)} %all-reduce.11.cloned.1.call-done) | copy-start | bytes 393220
  378.6 5.5 %copy-start.2 = (f32[1,1,1024,1024]{3,2,1,0:T(8,128)S(1)}, f32[1,1,1024,1024]{3,2,1,0:T(8,128)}, u32[]{:S(2)}) copy-start(f32[1,1,1024,1024]{3,2,1,0:T(8,128)} %param.12) | copy-start | bytes 12582916
  378.6 6.1 %copy-start.4 = (f32[1024,1024]{1,0:T(8,128)S(1)}, f32[1024,1024]{1,0:T(8,128)}, u32[]{:S(2)}) copy-start(f32[1024,1024]{1,0:T(8,128)} %copy-done.3) | copy-start | bytes 12582916
Sparse Core Ops, SparseCore 0:
  21.4 89.6 all-reduce.4
  119.4 36.0 all-reduce.6
  162.4 86.6 all-reduce.8
  257.4 36.1 all-reduce.10
  318.7 49.5 all-gather.2
where the time goes:
time: 398 us
  waiting for transfers between devices  249 us (63%)
  blocking collectives  65.7 us (17%)
  matrix products  42.2 us (11%)
  other arithmetic  19.3 us (5%)
  between operations  16 us (4%)
  local copies, waits for them, and re-layouts  5.77 us (1%)
    psum x2, waiting for transfers between devices, on_device(): left_sum = lax.psum(left_part, ('shard', 'tensor'))  176 us
    psum x2, waiting for transfers between devices, on_device(): right_part = lax.psum(right_local, 'shard') / shards  72.2 us
    all_gather x1, blocking collectives, on_device(): lax.all_gather(touched_grads, ('shard', 'section'), axis=0, tiled=True)  33.2 us
    all_gather x1, blocking collectives, on_device(): lax.all_gather(touched_ids, ('shard', 'section'), axis=0, tiled=True)  18.6 us
    psum x1, blocking collectives, on_device(): lax.psum(jnp.sum(gram_left * gram_right), ('tensor', 'section'))  14 us
    dot_general x2, matrix products, on_device(): lax.dot_general(right_part, corrected, (((1,), (1,)), ((), ())), precisio...  11.4 us
    dot_general x2, matrix products, on_device(): right_local = jnp.dot(left_unit, corrected, precision=highest)  11.2 us
    dot_general x1, matrix products, on_device(): lax.dot_general(out_grads[0], hidden_acts[0], (((0,), (0,)), ((), ())), p...  9.28 us
  transfers between devices with their start and end apart: 5, of which 4 were waited for; matrix products, arithmetic and copies ran while one was open for 4% of the time, Pallas kernels for 0%

commit v1 on v0

--- a/solution.py
+++ b/solution.py
@@ -48,7 +48,13 @@
         scaling = lax.rsqrt(jnp.sum(whitened * whitened) / rank_count + epsilon)
         left_unit = whitened * scaling
         right_local = jnp.dot(left_unit, corrected, precision=highest)
-        right_part = lax.psum(right_local, "shard") / shards
+
+        def cut_the_field(values, along_axis):
+            ready = jax.lax.all_gather(values, axis_name=along_axis)
+            main = jnp.sum(ready, axis=0)
+            return main
+
+        right_part = cut_the_field(right_local, "shard") / shards
     gram_left = jnp.dot(left_unit, left_unit.T, precision=highest)
     gram_right = jnp.dot(right_part, right_part.T, precision=highest)
     total_squares = lax.psum(jnp.sum(gram_left * gram_right), ("tensor", "section"))

time: 398 us -> 360 us (0.905)
  waiting for transfers between devices: 249 us -> 177 us
  blocking collectives: 65.7 us -> 101 us
    psum x2 -> x0, waiting for transfers between devices: 72.2 us -> none  [on_device(): right_part = lax.psum(right_local, 'shard') / shards]
    all_gather x0 -> x2, blocking collectives: none -> 34.5 us  [cut_the_field(): ready = jax.lax.all_gather(values, axis_name=along_axis)]
  transfers between devices with their start and end apart: 5 -> 3, of which waited for: 4 -> 2; matrix products, arithmetic and copies ran while one was open for 4% -> 5% of each run, Pallas kernels for 0% -> 0%
where the time goes in v1:
time: 360 us; the launch traced here: 359 us
  waiting for transfers between devices  177 us (49%)
  blocking collectives  101 us (28%)
  matrix products  40.3 us (11%)
  other arithmetic  21.4 us (6%)
  between operations  15.9 us (4%)
  local copies, waits for them, and re-layouts  3.75 us (1%)
    psum x2, waiting for transfers between devices, on_device(): left_sum = lax.psum(left_part, ('shard', 'tensor'))  177 us
    all_gather x2, blocking collectives, cut_the_field(): ready = jax.lax.all_gather(values, axis_name=along_axis)  34.5 us
    all_gather x1, blocking collectives, on_device(): lax.all_gather(touched_grads, ('shard', 'section'), axis=0, tiled=True)  33.1 us
    all_gather x1, blocking collectives, on_device(): lax.all_gather(touched_ids, ('shard', 'section'), axis=0, tiled=True)  19.5 us
    psum x1, blocking collectives, on_device(): lax.psum(jnp.sum(gram_left * gram_right), ('tensor', 'section'))  14 us
    dot_general x2, matrix products, on_device(): lax.dot_general(right_part, corrected, (((1,), (1,)), ((), ())), precisio...  11.4 us
    dot_general x2, matrix products, on_device(): right_local = jnp.dot(left_unit, corrected, precision=highest)  9.81 us
    dot_general x1, matrix products, on_device(): lax.dot_general(out_grads[0], hidden_acts[0], (((0,), (0,)), ((), ())), p...  9.28 us
  transfers between devices with their start and end apart: 3, of which 2 were waited for; matrix products, arithmetic and copies ran while one was open for 5% of the time, Pallas kernels for 0%

profile of v1, /device:TPU:0, one launch (start us, length us, event | category | flops | bytes accessed | tf_op | source)
XLA Modules:
  0.0 359.5 jit_solution(8757713297570547361)
XLA Ops:
  7.2 0.0 copy-start
  7.2 0.0 all-reduce.3.cloned.1.call-start
  7.2 0.0 copy-start.1
  7.2 9.3 %fusion.5 = bf16[1024,1024]{1,0:T(8,128)(2,1)S(1)} fusion(bf16[1,2560,1024]{2,1,0:T(8,128)(2,1)} %param.10, bf16[1,2560,1024]{2,1,0:T(8,128)(2,1)} %param.11), kind=kOutput, calls=%fused_computation.9 | convolution fusion | flops 5369757696 | bytes 12582912 | tf_op jit(solution)/shard_map/dot_general | solution.py:30
  16.5 0.0 copy-done
  16.5 0.0 copy-done.1
  16.5 0.0 copy-start.5
  16.6 4.7 %convolution_bitcast_fusion = f32[32,1024]{1,0:T(8,128)} fusion(f32[1,32,1024]{2,1,0:T(8,128)S(1)} %copy-done, f32[1,1,1024,1024]{3,2,1,0:T(8,128)S(1)} %copy-done.1, bf16[1024,1024]{1,0:T(8,128)(2,1)S(1)} %fusion.5), kind=kOutput, calls=%fused_computation.10 | convolution fusion | flops 404750336 | bytes 6553600 | tf_op jit(solution)/shard_map/dot_general | solution.py:39
  21.2 0.0 all-reduce.3.cloned.1.call-update
  21.3 0.0 all-reduce.5.cloned.1.call-start
  21.3 89.9 %all-reduce.3.cloned.1.call-done = f32[32,1024]{1,0:T(8,128)} async-done(((f32[32,1024]{1,0:T(8,128)}), f32[32,1024]{1,0:T(8,128)}) %all-reduce.3.cloned.1.call-update) | async-done | bytes 131088 | tf_op jit(solution)/shard_map/psum | solution.py:46
  111.2 0.0 copy-done.5
  111.2 1.8 multiply_reduce_fusion.1
  113.7 4.9 %fusion.15 = f32[32,1024]{1,0:T(8,128)S(1)} fusion(f32[1024,32]{0,1:T(8,128)S(1)} %get-tuple-element.10, f32[]{:T(128)S(6)} %rsqrt.7, f32[1,1,1024,1024]{3,2,1,0:T(8,128)} %param.12, bf16[1024,1024]{1,0:T(8,128)(2,1)S(1)} %fusion.5), kind=kOutput, calls=%fused_computation.20 | convolution fusion | flops 404783104 | bytes 6553604 | tf_op jit(solution)/shard_map/dot_general | solution.py:50
  118.7 17.3 %all-gather = f32[128,1024]{1,0:T(8,128)S(1)} all-gather(f32[32,1024]{1,0:T(8,128)S(1)} %fusion.15), channel_id=2, replica_groups=mesh['shard'=4,'tensor'=4,'section'=2] {'shard'}, dimensions={0}, use_global_device_ids=true | all-gather | bytes 655360 | tf_op jit(solution)/shard_map/all_gather | solution.py:53
  135.9 6.7 %fusion.13 = f32[32,1024]{1,0:T(8,128)} fusion(f32[32,1024]{1,0:T(8,128)S(1)} %reduce_sum.46, f32[1,1,1024,1024]{3,2,1,0:T(8,128)} %param.12, bf16[1024,1024]{1,0:T(8,128)(2,1)S(1)} %fusion.5), kind=kOutput, calls=%fused_computation.18 | convolution fusion | flops 404783104 | bytes 6553600 | tf_op jit(solution)/shard_map/dot_general | solution.py:39
  142.6 0.0 all-reduce.5.cloned.1.call-update
  142.7 0.2 all-gather.5.cloned.1.call-start
  142.9 86.7 %all-reduce.5.cloned.1.call-done = f32[32,1024]{1,0:T(8,128)} async-done(((f32[32,1024]{1,0:T(8,128)}), f32[32,1024]{1,0:T(8,128)}) %all-reduce.5.cloned.1.call-update) | async-done | bytes 131088 | tf_op jit(solution)/shard_map/psum | solution.py:46
  229.6 1.8 multiply_reduce_fusion
  232.1 0.3 fusion.20
  232.4 4.9 %fusion.23 = f32[32,1024]{1,0:T(8,128)S(1)} fusion(f32[1024,32]{0,1:T(8,128)S(1)} %get-tuple-element.12, f32[]{:T(128)S(6)} %rsqrt.8, f32[1,1,1024,1024]{3,2,1,0:T(8,128)} %param.12, bf16[1024,1024]{1,0:T(8,128)(2,1)S(1)} %fusion.5), kind=kOutput, calls=%fused_computation.30 | convolution fusion | flops 404783104 | bytes 6553604 | tf_op jit(solution)/shard_map/dot_general | solution.py:50
  237.3 17.3 %all-gather.1 = f32[128,1024]{1,0:T(8,128)S(1)} all-gather(f32[32,1024]{1,0:T(8,128)S(1)} %fusion.23), channel_id=3, replica_groups=mesh['shard'=4,'tensor'=4,'section'=2] {'shard'}, dimensions={0}, use_global_device_ids=true | all-gather | bytes 655360 | tf_op jit(solution)/shard_map/all_gather | solution.py:53
  254.6 0.9 fusion.11
  255.5 5.0 %fusion.18 = f32[1024,1024]{1,0:T(8,128)} fusion(f32[32,1024]{1,0:T(8,128)S(1)} %reduce_sum.48, f32[1024,32]{0,1:T(8,128)S(1)} %get-tuple-element.12, f32[]{:T(128)S(6)} %rsqrt.8), kind=kOutput, calls=%fused_computation.25 | convolution fusion | flops 402718720 | bytes 4456452 | tf_op jit(solution)/shard_map/dot_general | solution.py:61
  260.5 0.0 copy-start.6
  260.5 0.0 copy-start.4
  260.5 14.0 %psum.23 = f32[]{:T(128)} all-reduce(f32[]{:T(128)} %fusion.11), channel_id=1, replica_groups=mesh['shard'=4,'tensor'=4,'section'=2] {'tensor','section'}, use_global_device_ids=true, to_apply=%region_7.0 | all-reduce | flops 1 | bytes 8 | tf_op jit(solution)/shard_map/psum | solution.py:60
  275.2 3.9 %fusion.41 = (bf16[1,256,1024]{2,1,0:T(8,128)(2,1)}, f32[1,256,1024]{2,1,0:T(8,128)}, f32[1,256,1024]{2,1,0:T(8,128)}) fusion(f32[1,256,1024]{2,1,0:T(8,128)} %param.16, f32[1024,1024]{1,0:T(8,128)} %fusion.18, s32[]{:T(128)S(6)} %select_n.10, f32[]{:T(128)S(6)} %min_shard_map.3, f32[1,256,1024]{2,1,0:T(8,128)} %param.15), kind=kLoop, calls=%fused_computation.50 | loop fusion | flops 1572864 | bytes 5767176 | tf_op jit(solution)/shard_map/convert_element_type | solution.py:77
  279.1 0.0 all-gather.5.cloned.1.call-update
  279.2 0.0 copy-done.6
  279.2 19.5 %all-gather.2 = s32[8,1,128]{2,1,0:T(1,128)S(1)} all-gather(s32[1,1,128]{2,1,0:T(1,128)S(1)} %bitcast.52), channel_id=1, replica_groups=mesh['shard'=4,'tensor'=4,'section'=2] {'shard','section'}, dimensions={0}, use_global_device_ids=true | all-gather | bytes 4608 | tf_op jit(solution)/shard_map/all_gather | solution.py:84
  298.7 0.0 copy-done.4
  298.7 33.1 %all_gather.27 = bf16[1024,256]{1,0:T(8,128)(2,1)S(1)} all-gather(bf16[128,256]{1,0:T(8,128)(2,1)S(1)} %copy-done.4), channel_id=1, replica_groups=mesh['shard'=4,'tensor'=4,'section'=2] {'shard','section'}, dimensions={0}, use_global_device_ids=true | all-gather | bytes 589824 | tf_op jit(solution)/shard_map/all_gather | solution.py:83
  331.9 8.3 %scatter_custom_fusion = f32[4096,256]{1,0:T(8,128)} fusion(s32[1024]{0:T(1024)S(1)} %compare_select_fusion, f32[]{:T(128)} %constant.16.clone.1, bf16[1024,256]{1,0:T(8,128)(2,1)S(1)} %all_gather.27), kind=kCustom, calls=%fused_computation.7 | custom fusion | flops 524288 | bytes 4718596 | tf_op jit(solution)/shard_map/scatter-add | solution.py:92
  340.1 0.0 copy-start.2
  340.1 0.0 copy-start.3
  340.1 4.8 %subtract_convert_fusion = bf16[4096,256]{1,0:T(8,128)(2,1)} fusion(f32[4096,256]{1,0:T(8,128)} %scatter_custom_fusion, bf16[4096,256]{1,0:T(8,128)(2,1)} %param.17), kind=kLoop, calls=%fused_computation.5 | loop fusion | flops 4194304 | bytes 8388608 | tf_op jit(solution)/shard_map/convert_element_type | solution.py:94
  345.0 0.7 multiply_bitcast_fusion
  345.6 0.0 copy-done.2
  345.6 0.6 copy-done.3
  346.3 3.6 %subtract_bitcast_fusion = f32[1,1,1024,1024]{3,2,1,0:T(8,128)} fusion(f32[1024,1024]{1,0:T(8,128)S(1)} %copy-done.3, f32[1,1,1024,1024]{3,2,1,0:T(8,128)S(1)} %copy-done.2, bf16[1024,1024]{1,0:T(8,128)(2,1)S(1)} %fusion.5), kind=kLoop, calls=%fused_computation.6 | loop fusion | flops 3145728 | bytes 14680064 | tf_op jit(solution)/shard_map/broadcast_in_dim | solution.py:68
  349.9 0.0 all-gather.5.cloned.1.call-done
  349.9 3.1 copy.19
  (4 shorter events, 0.1 us)
Async XLA Ops:
  7.2 9.4 %copy-start = (f32[1,32,1024]{2,1,0:T(8,128)S(1)}, f32[1,32,1024]{2,1,0:T(8,128)}, u32[]{:S(2)}) copy-start(f32[1,32,1024]{2,1,0:T(8,128)} %param.13) | copy-start | bytes 393220
  7.2 104.0 %all-reduce.3.cloned.1.call-start = ((), (), s32[]{:S(2)}) async-start(), calls=%async_computation | async-start | bytes 262144 | tf_op jit(solution)/shard_map/psum | solution.py:46
  7.2 9.3 %copy-start.1 = (f32[1,1,1024,1024]{3,2,1,0:T(8,128)S(1)}, f32[1,1,1024,1024]{3,2,1,0:T(8,128)}, u32[]{:S(2)}) copy-start(f32[1,1,1024,1024]{3,2,1,0:T(8,128)} %param.12) | copy-start | bytes 12582916
  16.5 94.7 %copy-start.5 = (f32[1,2,32,32]{3,2,1,0:T(8,128)S(1)}, f32[1,2,32,32]{3,2,1,0:T(8,128)}, u32[]{:S(2)}) copy-start(f32[1,2,32,32]{3,2,1,0:T(8,128)} %param.14) | copy-start | bytes 24580
  21.3 208.3 %all-reduce.5.cloned.1.call-start = ((), (), s32[]{:S(2)}) async-start(), calls=%async_computation.1 | async-start | bytes 262144 | tf_op jit(solution)/shard_map/psum | solution.py:46
  142.7 207.2 %all-gather.5.cloned.1.call-start = ((), (), s32[]{:S(2)}) async-start(), calls=%async_computation.2 | async-start | bytes 2621440 | tf_op jit(solution)/shard_map/all_gather | solution.py:77
  260.5 18.7 %copy-start.6 = (s32[128]{0:T(128)S(1)}, s32[128]{0:T(128)}, u32[]{:S(2)}) copy-start(s32[128]{0:T(128)} %param.18) | copy-start | bytes 1540
  260.5 38.2 %copy-start.4 = (bf16[128,256]{1,0:T(8,128)(2,1)S(1)}, bf16[128,256]{1,0:T(8,128)(2,1)}, u32[]{:S(2)}) copy-start(bf16[128,256]{1,0:T(8,128)(2,1)} %param.19) | copy-start | bytes 196612
  340.1 5.5 %copy-start.2 = (f32[1,1,1024,1024]{3,2,1,0:T(8,128)S(1)}, f32[1,1,1024,1024]{3,2,1,0:T(8,128)}, u32[]{:S(2)}) copy-start(f32[1,1,1024,1024]{3,2,1,0:T(8,128)} %param.12) | copy-start | bytes 12582916
  340.1 6.1 %copy-start.3 = (f32[1024,1024]{1,0:T(8,128)S(1)}, f32[1024,1024]{1,0:T(8,128)}, u32[]{:S(2)}) copy-start(f32[1024,1024]{1,0:T(8,128)} %fusion.18) | copy-start | bytes 12582916
Sparse Core Ops, SparseCore 0:
  21.4 89.7 all-reduce.2
  142.8 86.7 all-reduce.4
  279.3 49.7 all-gather.4
